TPU v7x, 128 devices: a whole 4x4x4 slice. The times are simulated.
128 devices in a mesh: dp: 4 (over z), expert: 32 (over x, y, core).
Axes of the slice: x: 4, y: 4, z: 4, core: 2. Of those that a mesh axis runs over, the one named last changes fastest.
Arguments:
- grad_parts: bfloat16 [4, 128, 128, 2048], P('dp', 'expert'), may hold values from -6 to 6
- first_moment: float32 [128, 128, 2048], P('expert', None, 'dp'), may hold values from -4 to 4
- second_moment: float32 [128, 128, 2048], P('expert', None, 'dp'), may hold values from 0.05 to 2
- master_weight: float32 [128, 128, 2048], P('expert', None, 'dp'), may hold values from -6 to 6
- old_owner: int32 [104], replicated, may hold values from 0 to 25, as said below
- new_owner: int32 [104], replicated, may hold values from 0 to 31, as said below
Outputs:
- new_master: float32 [192, 128, 2048], P('expert', None, 'dp')
- new_first: float32 [192, 128, 2048], P('expert', None, 'dp')
- new_second: float32 [192, 128, 2048], P('expert', None, 'dp')
- new_params: bfloat16 [192, 128, 2048], P('expert')
Inputs may be any that keep to these rules, and one draw needn't show every extreme that they name: `old_owner`: tiles are owned by devices 0 to 25 of the expert axis, exactly 4 each; the other devices own none, and their slots of the old-layout arrays are never read. `new_owner`: each device owns at most 6 tiles and some own exactly 6; the tiles of one old owner go to different new owners.
All inputs are finite; a program needn't handle non-finite values.
Results may differ from a plain program's by a relative error of at most 0.0085.
Values may be sent and summed in bfloat16 or wider, within the bound.
No kernel may reach another device: no remote copies, remote signals or barrier semaphores. Data moves between devices by JAX's collectives and lax.ppermute only.
A program may use at most 128 MiB of HBM per device.

v0:
```python
import jax
import jax.numpy as jnp
from jax import lax
from jax.sharding import PartitionSpec as P


def slot_ranks(owner, count):
    matches = (owner[:, None] == jnp.arange(count, dtype=jnp.int32)[None, :]).astype(jnp.int32)
    before = jnp.cumsum(matches, axis=0) - matches
    return jnp.sum(before * matches, axis=1)


def adam_step(gradient, moment_one, moment_two, weight):
    moment_one = 0.9 * moment_one + 0.1 * gradient
    moment_two = 0.95 * moment_two + 0.05 * gradient * gradient
    update = moment_one / (1.0 - 0.9**50) / (jnp.sqrt(moment_two / (1.0 - 0.95**50)) + 1e-08)
    weight = weight - 0.05 * (update + 0.1 * weight)
    return (weight, moment_one, moment_two)


def shards(grad_parts, first_moment, second_moment, master_weight, old_owner, new_owner):
    peer_count = lax.axis_size("expert")
    device = lax.axis_index("expert")
    old_slots = first_moment.shape[0]
    new_slots = min(old_slots + old_slots // 2, peer_count - peer_count // 5)
    old_rank = slot_ranks(old_owner, peer_count)
    new_rank = slot_ranks(new_owner, peer_count)
    targets = jnp.arange(peer_count, dtype=jnp.int32)
    outgoing = (old_owner == device)[:, None] & (new_owner[:, None] == targets[None, :])
    send_has = jnp.sum(outgoing.astype(jnp.int32), axis=0) > 0
    send_slot = jnp.sum(jnp.where(outgoing, old_rank[:, None], 0), axis=0)
    slot_ids = jnp.arange(new_slots, dtype=jnp.int32)
    wanted = (new_owner == device)[:, None] & (new_rank[:, None] == slot_ids[None, :])
    recv_has = jnp.sum(wanted.astype(jnp.int32), axis=0) > 0
    recv_source = jnp.sum(jnp.where(wanted, old_owner[:, None], 0), axis=0)

    def to_peers(values):
        return jnp.where(send_has[:, None, None], values[send_slot], 0.0)

    def from_peers(values):
        return jnp.where(recv_has[:, None, None], values[recv_source], 0.0)

    summed = lax.psum_scatter(grad_parts[0], "dp", scatter_dimension=2, tiled=True).astype(
        jnp.float32
    )
    weight, moment_one, moment_two = adam_step(summed, first_moment, second_moment, master_weight)
    results = (
        lax.all_to_all(
            to_peers(weight).astype(jnp.bfloat16), "expert", split_axis=0, concat_axis=0, tiled=True
        ).astype(jnp.float32),
        lax.all_to_all(
            to_peers(moment_one).astype(jnp.bfloat16),
            "expert",
            split_axis=0,
            concat_axis=0,
            tiled=True,
        ).astype(jnp.float32),
        lax.all_to_all(
            to_peers(moment_two).astype(jnp.bfloat16),
            "expert",
            split_axis=0,
            concat_axis=0,
            tiled=True,
        ).astype(jnp.float32),
    )
    new_master = from_peers(results[0])
    new_first = from_peers(results[1])
    new_second = from_peers(results[2])
    new_params = lax.all_gather(new_master.astype(jnp.bfloat16), "dp", axis=2, tiled=True)
    return (new_master, new_first, new_second, new_params)


def solution(mesh):
    placed = (
        P("dp", "expert", None, None),
        P("expert", None, "dp"),
        P("expert", None, "dp"),
        P("expert", None, "dp"),
        P(),
        P(),
    )
    return jax.shard_map(
        shards,
        mesh=mesh,
        in_specs=placed,
        out_specs=(
            P("expert", None, "dp"),
            P("expert", None, "dp"),
            P("expert", None, "dp"),
            P("expert", None, None),
        ),
        check_vma=False,
    )
```

profile of v0, /device:TPU:1, one launch (start us, length us, event | category | flops | bytes accessed | tf_op | source)
XLA Modules:
  0.0 297.9 jit_solution(7554008019410971334)
XLA Ops:
  7.2 0.0 reduce-scatter.2.cloned.1.call-start
  7.2 0.7 reduce-scatter.2.cloned.1.call-update
  7.9 0.7 fusion.2
  8.6 0.1 reduce_window_sum.18
  8.8 0.7 fusion.4
  9.5 0.1 reduce_window_sum.17
  9.7 0.8 select_reduce_fusion.1
  10.5 0.7 broadcast_compare_fusion.2
  11.2 0.9 convert_reduce_fusion
  12.1 31.5 %reduce-scatter.2.cloned.1.call-done = bf16[4,128,512]{2,1,0:T(8,128)(2,1)} async-done(((bf16[4,128,2048]{2,1,0:T(8,128)(2,1)}), bf16[4,128,512]{2,1,0:T(8,128)(2,1)}) %reduce-scatter.2.cloned.1.call-update) | async-done | bytes 524304 | tf_op jit(solution)/shard_map/reduce_scatter | solution.py:43
  43.6 3.0 multiply_subtract_fusion
  46.6 2.8 gather_fusion
  49.3 2.7 gather_fusion.2
  52.1 2.8 gather_fusion.4
  54.9 7.9 %select_convert_fusion = (bf16[32,128,512]{2,1,0:T(8,128)(2,1)}, bf16[32,128,512]{2,1,0:T(8,128)(2,1)S(1)}, bf16[32,128,512]{2,1,0:T(8,128)(2,1)S(1)}) fusion(bf16[32,128,512]{2,1,0:T(8,128)(2,1)} %gather_fusion.4, pred[32]{0:T(512)(128)(4,1)S(1)} %broadcast_compare_fusion, bf16[32,128,512]{2,1,0:T(8,128)(2,1)} %gather_fusion.2, ...), kind=kLoop, calls=%fused_computation.6 | loop fusion | flops 6291456 | bytes 25165856 | tf_op jit(solution)/shard_map/convert_element_type | solution.py:59
  62.8 58.0 %all_to_all.15 = bf16[32,128,512]{2,1,0:T(8,128)(2,1)} all-to-all(bf16[32,128,512]{2,1,0:T(8,128)(2,1)S(1)} %get-tuple-element.20), channel_id=1, replica_groups=mesh['dp'=4,'expert'=32] {'expert'}, dimensions={0} | all-to-all | bytes 8388608 | tf_op jit(solution)/shard_map/all_to_all | solution.py:48
  120.7 54.5 %all_to_all.16 = bf16[32,128,512]{2,1,0:T(8,128)(2,1)} all-to-all(bf16[32,128,512]{2,1,0:T(8,128)(2,1)S(1)} %get-tuple-element.19), channel_id=1, replica_groups=mesh['dp'=4,'expert'=32] {'expert'}, dimensions={0} | all-to-all | bytes 8388608 | tf_op jit(solution)/shard_map/all_to_all | solution.py:51
  175.2 0.0 copy-start
  175.2 4.8 %all-to-all-start.2 = ((bf16[32,128,512]{2,1,0:T(8,128)(2,1)}), bf16[32,128,512]{2,1,0:T(8,128)(2,1)}, u32[]{:S(2)}, u32[]{:S(2)}) async-start(bf16[32,128,512]{2,1,0:T(8,128)(2,1)} %get-tuple-element.18), calls=%async_computation.3 | async-start | bytes 8388608 | tf_op jit(solution)/shard_map/all_to_all | solution.py:58
  180.0 0.0 all-gather.2.cloned.1.call-start
  180.0 0.0 copy-done
  180.0 0.1 convert_reduce_fusion.1
  180.2 6.6 %convert_element_type.42 = f32[32,128,512]{2,1,0:T(8,128)} convert(bf16[32,128,512]{2,1,0:T(8,128)(2,1)} %all_to_all.15) | non-fusion elementwise | flops 2097152 | bytes 12582912 | tf_op jit(solution)/shard_map/convert_element_type | solution.py:50
  186.8 4.0 %gather_fusion.1 = f32[6,128,512]{2,1,0:T(8,128)S(1)} fusion(f32[32,128,512]{2,1,0:T(8,128)} %convert_element_type.42, s32[1024]{0:T(1024)S(1)} %pad_clamp_fusion), kind=kCustom, calls=%fused_computation.1 | custom fusion | bytes 3145752 | tf_op jit(solution)/shard_map/gather | solution.py:41
  190.8 6.6 %convert_element_type.44 = f32[32,128,512]{2,1,0:T(8,128)} convert(bf16[32,128,512]{2,1,0:T(8,128)(2,1)} %all_to_all.16) | non-fusion elementwise | flops 2097152 | bytes 12582912 | tf_op jit(solution)/shard_map/convert_element_type | solution.py:57
  197.4 4.0 %gather_fusion.3 = f32[6,128,512]{2,1,0:T(8,128)S(1)} fusion(f32[32,128,512]{2,1,0:T(8,128)} %convert_element_type.44, s32[1024]{0:T(1024)S(1)} %pad_clamp_fusion), kind=kCustom, calls=%fused_computation.3 | custom fusion | bytes 3145752 | tf_op jit(solution)/shard_map/gather | solution.py:41
  201.4 30.8 %all-to-all-done.2 = bf16[32,128,512]{2,1,0:T(8,128)(2,1)} async-done(((bf16[32,128,512]{2,1,0:T(8,128)(2,1)}), bf16[32,128,512]{2,1,0:T(8,128)(2,1)}, u32[]{:S(2)}, u32[]{:S(2)}) %all-to-all-start.2) | async-done | bytes 4194336 | tf_op jit(solution)/shard_map/all_to_all | solution.py:58
  232.2 6.6 %convert_element_type.46 = f32[32,128,512]{2,1,0:T(8,128)} convert(bf16[32,128,512]{2,1,0:T(8,128)(2,1)} %all-to-all-done.2) | non-fusion elementwise | flops 2097152 | bytes 12582912 | tf_op jit(solution)/shard_map/convert_element_type | solution.py:64
  238.8 5.2 %gather_fusion.5 = f32[6,128,512]{2,1,0:T(8,128)} fusion(f32[32,128,512]{2,1,0:T(8,128)} %convert_element_type.46, s32[1024]{0:T(1024)S(1)} %pad_clamp_fusion), kind=kCustom, calls=%fused_computation.5 | custom fusion | bytes 3145752 | tf_op jit(solution)/shard_map/gather | solution.py:41
  243.9 4.1 %broadcast_select_fusion = (f32[6,128,512]{2,1,0:T(8,128)}, f32[6,128,512]{2,1,0:T(8,128)}, bf16[6,128,512]{2,1,0:T(8,128)(2,1)}, f32[6,128,512]{2,1,0:T(8,128)}) fusion(f32[6,128,512]{2,1,0:T(8,128)} %gather_fusion.5, pred[6]{0:T(512)(128)(4,1)S(1)} %broadcast_compare_fusion.1, f32[6,128,512]{2,1,0:T(8,128)S(1)} %gather_fusion.3, ...), kind=kLoop, calls=%fused_computation.14 | loop fusion | flops 1572864 | bytes 10223622 | tf_op jit(solution)/shard_map/jit(_where)/select_n | solution.py:41
  248.0 0.0 all-gather.2.cloned.1.call-update
  248.1 39.1 %all-gather.2.cloned.1.call-done = bf16[6,128,2048]{2,1,0:T(8,128)(2,1)} async-done(((bf16[6,128,512]{2,1,0:T(8,128)(2,1)}), bf16[6,128,2048]{2,1,0:T(8,128)(2,1)}) %all-gather.2.cloned.1.call-update) | async-done | bytes 3145744 | tf_op jit(solution)/shard_map/all_gather | solution.py:69
  287.1 4.0 %copy.11 = bf16[6,128,2048]{2,1,0:T(8,128)(2,1)} copy(bf16[6,128,2048]{2,1,0:T(8,128)(2,1)} %all-gather.2.cloned.1.call-done) | data formatting | bytes 6291456
  (6 shorter events, 0.0 us)
Async XLA Ops:
  7.2 36.4 %reduce-scatter.2.cloned.1.call-start = ((), (), s32[]{:S(2)}) async-start(), calls=%async_computation.4 | async-start | bytes 2621440 | tf_op jit(solution)/shard_map/reduce_scatter | solution.py:43
  175.2 4.8 %copy-start = (s32[104]{0:T(128)S(1)}, s32[104]{0:T(128)}, u32[]{:S(2)}) copy-start(s32[104]{0:T(128)} %param.10) | copy-start | bytes 1252
  175.2 57.0 %all-to-all-start.2 = ((bf16[32,128,512]{2,1,0:T(8,128)(2,1)}), bf16[32,128,512]{2,1,0:T(8,128)(2,1)}, u32[]{:S(2)}, u32[]{:S(2)}) async-start(bf16[32,128,512]{2,1,0:T(8,128)(2,1)} %get-tuple-element.18), calls=%async_computation.3 | async-start | bytes 8388608 | tf_op jit(solution)/shard_map/all_to_all | solution.py:58
  180.0 107.2 %all-gather.2.cloned.1.call-start = ((), (), s32[]{:S(2)}) async-start(), calls=%async_computation.5 | async-start | bytes 3932160 | tf_op jit(solution)/shard_map/all_gather | solution.py:69
Sparse Core Ops, SparseCore 0:
  10.4 33.1 reduce-scatter.1
  248.2 38.9 all-gather.1
where the time goes:
time: 299 us; the launch traced here: 298 us
  blocking collectives  112 us (37%)
  waiting for transfers between devices  102 us (34%)
  other arithmetic  39 us (13%)
  local copies, waits for them, and re-layouts  25.5 us (9%)
  between operations  14.1 us (5%)
  starting transfers between devices  4.85 us (2%)
    all_to_all x1, blocking collectives, shards(): lax.all_to_all(to_peers(weight).astype(jnp.bfloat16), 'expert', split_axi...  58 us
    all_to_all x1, blocking collectives, shards(): lax.all_to_all(to_peers(moment_one).astype(jnp.bfloat16), 'expert', split...  54.5 us
    all_gather x1, waiting for transfers between devices, shards(): lax.all_gather(new_master.astype(jnp.bfloat16), 'dp', axis=2, tiled=True)  39.1 us
    reduce_scatter x1, waiting for transfers between devices, shards(): lax.psum_scatter(grad_parts[0], 'dp', scatter_dimension=2, tiled=True)  31.5 us
    all_to_all x1, waiting for transfers between devices, shards(): lax.all_to_all(to_peers(moment_two).astype(jnp.bfloat16), 'expert', split...  30.8 us
    convert_element_type x3, other arithmetic, shards(): results = (lax.all_to_all(to_peers(weight).astype(jnp.bfloat16), 'expert'...  19.7 us
    gather x3, local copies, waits for them, and re-layouts, from_peers(): return jnp.where(recv_has[:, None, None], values[recv_source], 0.0)  13.2 us
    gather x3, local copies, waits for them, and re-layouts, to_peers(): return jnp.where(send_has[:, None, None], values[send_slot], 0.0)  8.3 us
  transfers between devices with their start and end apart: 3, of which 3 were waited for; matrix products, arithmetic and copies ran while one was open for 9% of the time, Pallas kernels for 0%

commit v1 on v0

--- a/solution.py
+++ b/solution.py
@@ -2,6 +2,11 @@
 import jax.numpy as jnp
 from jax import lax
 from jax.sharding import PartitionSpec as P
+
+
+def gather_over(x, name, d):
+    repeated = jnp.stack([x] * lax.axis_size(name))
+    return jnp.concatenate(lax.all_to_all(repeated, name, 0, 0), axis=d)
 
 
 def slot_ranks(owner, count):
@@ -66,7 +71,7 @@
     new_master = from_peers(results[0])
     new_first = from_peers(results[1])
     new_second = from_peers(results[2])
-    new_params = lax.all_gather(new_master.astype(jnp.bfloat16), "dp", axis=2, tiled=True)
+    new_params = gather_over(new_master.astype(jnp.bfloat16), "dp", 2)
     return (new_master, new_first, new_second, new_params)
 
 

time: 299 us -> 305 us (1.020)
  blocking collectives: 112 us -> 152 us
  waiting for transfers between devices: 102 us -> 63 us
  local copies, waits for them, and re-layouts: 25.5 us -> 29.3 us
    all_to_all x0 -> x1, blocking collectives: none -> 39.1 us  [gather_over(): return jnp.concatenate(lax.all_to_all(repeated, name, 0, 0), axis=d)]
    all_gather x1 -> x0, waiting for transfers between devices: 39.1 us -> none  [shards(): lax.all_gather(new_master.astype(jnp.bfloat16), 'dp', axis=2, tiled=True)]
  transfers between devices with their start and end apart: 3 -> 2, of which waited for: 3 -> 2; matrix products, arithmetic and copies ran while one was open for 9% -> 8% of each run, Pallas kernels for 0% -> 0%
where the time goes in v1:
time: 305 us; the launch traced here: 302 us
  blocking collectives  152 us (50%)
  waiting for transfers between devices  63 us (21%)
  other arithmetic  38.7 us (13%)
  local copies, waits for them, and re-layouts  29.3 us (10%)
  between operations  14.1 us (5%)
  starting transfers between devices  4.81 us (2%)
    all_to_all x1, blocking collectives, shards(): lax.all_to_all(to_peers(weight).astype(jnp.bfloat16), 'expert', split_axi...  58 us
    all_to_all x1, blocking collectives, shards(): lax.all_to_all(to_peers(moment_one).astype(jnp.bfloat16), 'expert', split...  54.5 us
    all_to_all x1, blocking collectives, gather_over(): return jnp.concatenate(lax.all_to_all(repeated, name, 0, 0), axis=d)  39.1 us
    reduce_scatter x1, waiting for transfers between devices, shards(): lax.psum_scatter(grad_parts[0], 'dp', scatter_dimension=2, tiled=True)  31.5 us
    all_to_all x1, waiting for transfers between devices, shards(): lax.all_to_all(to_peers(moment_two).astype(jnp.bfloat16), 'expert', split...  30.9 us
    convert_element_type x3, other arithmetic, shards(): results = (lax.all_to_all(to_peers(weight).astype(jnp.bfloat16), 'expert'...  19.7 us
    gather x3, local copies, waits for them, and re-layouts, from_peers(): return jnp.where(recv_has[:, None, None], values[recv_source], 0.0)  13.2 us
    gather x3, local copies, waits for them, and re-layouts, to_peers(): return jnp.where(send_has[:, None, None], values[send_slot], 0.0)  8.3 us
  transfers between devices with their start and end apart: 2, of which 2 were waited for; matrix products, arithmetic and copies ran while one was open for 8% of the time, Pallas kernels for 0%

profile of v1, /device:TPU:1, one launch (start us, length us, event | category | flops | bytes accessed | tf_op | source)
XLA Modules:
  0.0 301.6 jit_solution(12725838400021941493)
XLA Ops:
  7.2 0.0 reduce-scatter.2.cloned.1.call-start
  7.2 0.7 reduce-scatter.2.cloned.1.call-update
  7.9 0.7 fusion.2
  8.6 0.1 reduce_window_sum.18
  8.8 0.7 fusion.4
  9.5 0.1 reduce_window_sum.17
  9.7 0.8 select_reduce_fusion.1
  10.5 0.7 broadcast_compare_fusion.2
  11.2 0.9 convert_reduce_fusion
  12.1 31.5 %reduce-scatter.2.cloned.1.call-done = bf16[4,128,512]{2,1,0:T(8,128)(2,1)} async-done(((bf16[4,128,2048]{2,1,0:T(8,128)(2,1)}), bf16[4,128,512]{2,1,0:T(8,128)(2,1)}) %reduce-scatter.2.cloned.1.call-update) | async-done | bytes 524304 | tf_op jit(solution)/shard_map/reduce_scatter | solution.py:48
  43.6 3.0 multiply_subtract_fusion
  46.6 2.8 gather_fusion
  49.3 2.7 gather_fusion.2
  52.1 2.8 gather_fusion.4
  54.9 7.9 %select_convert_fusion = (bf16[32,128,512]{2,1,0:T(8,128)(2,1)}, bf16[32,128,512]{2,1,0:T(8,128)(2,1)S(1)}, bf16[32,128,512]{2,1,0:T(8,128)(2,1)S(1)}) fusion(bf16[32,128,512]{2,1,0:T(8,128)(2,1)} %gather_fusion.4, pred[32]{0:T(512)(128)(4,1)S(1)} %broadcast_compare_fusion, bf16[32,128,512]{2,1,0:T(8,128)(2,1)} %gather_fusion.2, ...), kind=kLoop, calls=%fused_computation.6 | loop fusion | flops 6291456 | bytes 25165856 | tf_op jit(solution)/shard_map/convert_element_type | solution.py:64
  62.8 58.0 %all_to_all.20 = bf16[32,128,512]{2,1,0:T(8,128)(2,1)} all-to-all(bf16[32,128,512]{2,1,0:T(8,128)(2,1)S(1)} %get-tuple-element.28), channel_id=1, replica_groups=mesh['dp'=4,'expert'=32] {'expert'}, dimensions={0} | all-to-all | bytes 8388608 | tf_op jit(solution)/shard_map/all_to_all | solution.py:53
  120.7 54.5 %all_to_all.21 = bf16[32,128,512]{2,1,0:T(8,128)(2,1)} all-to-all(bf16[32,128,512]{2,1,0:T(8,128)(2,1)S(1)} %get-tuple-element.27), channel_id=1, replica_groups=mesh['dp'=4,'expert'=32] {'expert'}, dimensions={0} | all-to-all | bytes 8388608 | tf_op jit(solution)/shard_map/all_to_all | solution.py:56
  175.2 0.0 copy-start
  175.2 4.8 %all-to-all-start.2 = ((bf16[32,128,512]{2,1,0:T(8,128)(2,1)}), bf16[32,128,512]{2,1,0:T(8,128)(2,1)}, u32[]{:S(2)}, u32[]{:S(2)}) async-start(bf16[32,128,512]{2,1,0:T(8,128)(2,1)} %get-tuple-element.26), calls=%async_computation.3 | async-start | bytes 8388608 | tf_op jit(solution)/shard_map/all_to_all | solution.py:63
  180.0 0.0 copy-done
  180.0 0.1 convert_reduce_fusion.1
  180.2 6.6 %convert_element_type.44 = f32[32,128,512]{2,1,0:T(8,128)} convert(bf16[32,128,512]{2,1,0:T(8,128)(2,1)} %all_to_all.20) | non-fusion elementwise | flops 2097152 | bytes 12582912 | tf_op jit(solution)/shard_map/convert_element_type | solution.py:55
  186.7 4.0 %gather_fusion.1 = f32[6,128,512]{2,1,0:T(8,128)S(1)} fusion(f32[32,128,512]{2,1,0:T(8,128)} %convert_element_type.44, s32[1024]{0:T(1024)S(1)} %pad_clamp_fusion), kind=kCustom, calls=%fused_computation.1 | custom fusion | bytes 3145752 | tf_op jit(solution)/shard_map/gather | solution.py:46
  190.8 6.6 %convert_element_type.46 = f32[32,128,512]{2,1,0:T(8,128)} convert(bf16[32,128,512]{2,1,0:T(8,128)(2,1)} %all_to_all.21) | non-fusion elementwise | flops 2097152 | bytes 12582912 | tf_op jit(solution)/shard_map/convert_element_type | solution.py:62
  197.3 4.0 %gather_fusion.3 = f32[6,128,512]{2,1,0:T(8,128)S(1)} fusion(f32[32,128,512]{2,1,0:T(8,128)} %convert_element_type.46, s32[1024]{0:T(1024)S(1)} %pad_clamp_fusion), kind=kCustom, calls=%fused_computation.3 | custom fusion | bytes 3145752 | tf_op jit(solution)/shard_map/gather | solution.py:46
  201.3 30.9 %all-to-all-done.2 = bf16[32,128,512]{2,1,0:T(8,128)(2,1)} async-done(((bf16[32,128,512]{2,1,0:T(8,128)(2,1)}), bf16[32,128,512]{2,1,0:T(8,128)(2,1)}, u32[]{:S(2)}, u32[]{:S(2)}) %all-to-all-start.2) | async-done | bytes 4194336 | tf_op jit(solution)/shard_map/all_to_all | solution.py:63
  232.2 6.6 %convert_element_type.48 = f32[32,128,512]{2,1,0:T(8,128)} convert(bf16[32,128,512]{2,1,0:T(8,128)(2,1)} %all-to-all-done.2) | non-fusion elementwise | flops 2097152 | bytes 12582912 | tf_op jit(solution)/shard_map/convert_element_type | solution.py:69
  238.8 5.2 %gather_fusion.5 = f32[6,128,512]{2,1,0:T(8,128)} fusion(f32[32,128,512]{2,1,0:T(8,128)} %convert_element_type.48, s32[1024]{0:T(1024)S(1)} %pad_clamp_fusion), kind=kCustom, calls=%fused_computation.5 | custom fusion | bytes 3145752 | tf_op jit(solution)/shard_map/gather | solution.py:46
  243.9 3.9 %broadcast_select_fusion = (f32[6,128,512]{2,1,0:T(8,128)}, f32[6,128,512]{2,1,0:T(8,128)}, bf16[6,128,512]{2,1,0:T(8,128)(2,1)S(1)}, f32[6,128,512]{2,1,0:T(8,128)}) fusion(f32[6,128,512]{2,1,0:T(8,128)} %gather_fusion.5, pred[6]{0:T(512)(128)(4,1)S(1)} %broadcast_compare_fusion.1, f32[6,128,512]{2,1,0:T(8,128)S(1)} %gather_fusion.3, ...), kind=kLoop, calls=%fused_computation.14 | loop fusion | flops 1572864 | bytes 10223622 | tf_op jit(solution)/shard_map/jit(_where)/select_n | solution.py:46
  247.8 0.3 stack.2
  248.1 39.1 %all_to_all.22 = bf16[4,6,128,512]{3,2,1,0:T(8,128)(2,1)S(1)} all-to-all(bf16[4,6,128,512]{3,2,1,0:T(8,128)(2,1)S(1)} %stack.2), channel_id=1, replica_groups=mesh['dp'=4,'expert'=32] {'dp'}, dimensions={0} | all-to-all | bytes 6291456 | tf_op jit(solution)/shard_map/all_to_all | solution.py:9
  287.3 2.8 copy.12
  290.1 4.6 %copy.13 = bf16[6,128,2048]{2,1,0:T(8,128)(2,1)} copy(bf16[6,128,2048]{1,2,0:T(8,128)(2,1)} %bitcast.12) | data formatting | bytes 6291456
  (6 shorter events, 0.0 us)
Async XLA Ops:
  7.2 36.4 %reduce-scatter.2.cloned.1.call-start = ((), (), s32[]{:S(2)}) async-start(), calls=%async_computation.5 | async-start | bytes 2621440 | tf_op jit(solution)/shard_map/reduce_scatter | solution.py:48
  175.2 4.8 %copy-start = (s32[104]{0:T(128)S(1)}, s32[104]{0:T(128)}, u32[]{:S(2)}) copy-start(s32[104]{0:T(128)} %param.10) | copy-start | bytes 1252
  175.2 57.0 %all-to-all-start.2 = ((bf16[32,128,512]{2,1,0:T(8,128)(2,1)}), bf16[32,128,512]{2,1,0:T(8,128)(2,1)}, u32[]{:S(2)}, u32[]{:S(2)}) async-start(bf16[32,128,512]{2,1,0:T(8,128)(2,1)} %get-tuple-element.26), calls=%async_computation.3 | async-start | bytes 8388608 | tf_op jit(solution)/shard_map/all_to_all | solution.py:63
Sparse Core Ops, SparseCore 0:
  10.4 33.1 reduce-scatter.1
